TPU v7x, 128 devices: a whole 4x4x4 slice. The times are simulated.
128 devices in a mesh: aux: 8 (over x, core), basis: 16 (over z, y).
Axes of the slice: x: 4, y: 4, z: 4, core: 2. Of those that a mesh axis runs over, the one named last changes fastest.
Arguments:
- v_blocks: bfloat16 [64, 768, 128, 128], P('aux', 'basis'), may hold values from -6 to 6
- pair_map: int32 [8, 768, 2], P('aux', 'basis'), may hold values from 0 to 239, as said below
- pair_count: int32 [8, 16], P('aux', 'basis'), may hold values from 2 to 48, as said below
- occ_coef: bfloat16 [8, 30720], P(None, 'basis'), may hold values from -0.375 to 0.375
- virt_coef: bfloat16 [30720, 32768], P('basis', 'aux'), may hold values from -0.03125 to 0.03125
Outputs:
- b_tensor: bfloat16 [32768, 512], P(('aux', 'basis'))
Inputs may be any that keep to these rules, and one draw needn't show every extreme that they name: pair_map[s, k, 0] lies in the blocks of basis index k // 48 (blocks b * 240 / 16 onward); pair_map[s, k, 1] lies within 8 blocks of it, cyclically over 240 blocks, and that distance 8 is reached. Only the first pair_count slots of a device are live; in every slab some basis index has all 48 live.
All inputs are finite; a program needn't handle non-finite values.
Results may differ from a plain program's by a relative error of at most 0.0049.
Values may be sent and summed in bfloat16 or wider, within the bound.
A program may use at most 192 MiB of HBM per device.

v0:
```python
import jax
import jax.numpy as jnp
from jax import lax
from jax.sharding import PartitionSpec as P

BB = 128
NOCC = 8
NEAR = 8
PAIR_CAP = 48
NB = 240


def extended(array, sides, width):
    for axis, dim in sides:
        peers, length = (lax.axis_size(axis), array.shape[dim])
        up = [(i, (i + 1) % peers) for i in range(peers)]
        down = [(j, i) for i, j in up]
        last = lax.slice_in_dim(array, length - width, length, axis=dim)
        initial = lax.slice_in_dim(array, 0, width, axis=dim)
        before = lax.ppermute(last, axis, up)
        after = lax.ppermute(initial, axis, down)
        array = jnp.concatenate([before, array, after], axis=dim)
    return array


def local(v_blocks, pair_map, pair_count, occ_coef, virt_coef):
    blocks_here = virt_coef.shape[0] // BB
    device = lax.axis_index("basis")
    first_block = device * blocks_here
    mu_block = pair_map[0, :, 0]
    nu_block = pair_map[0, :, 1]
    padded = extended(occ_coef, (("basis", 1),), NEAR * BB)
    occ_table = padded.reshape(NOCC, blocks_here + 2 * NEAR, BB)
    position = jnp.mod(nu_block - first_block + NEAR, NB)
    picked = jnp.take(occ_table, position, axis=1)
    live_slots = (jnp.arange(PAIR_CAP) < pair_count[0, 0]).astype(jnp.float32)
    half_sums = jnp.einsum("qkmn,ikn->qikm", v_blocks, picked, preferred_element_type=jnp.float32)
    half_sums = half_sums * live_slots[None, None, :, None]
    owner_map = ((mu_block - first_block)[:, None] == jnp.arange(blocks_here)[None, :]).astype(
        jnp.float32
    )
    local_half = jnp.einsum("qikm,kb->qibm", half_sums, owner_map, precision=lax.Precision.HIGHEST)
    half_rows = local_half.reshape(v_blocks.shape[0] * NOCC, blocks_here * BB).astype(jnp.bfloat16)
    gathered = lax.all_gather(half_rows, "aux", axis=0, tiled=True)
    result = lax.psum_scatter(
        lax.dot_general(
            virt_coef, gathered, (((0,), (1,)), ((), ())), preferred_element_type=jnp.float32
        ),
        "basis",
        scatter_dimension=0,
        tiled=True,
    )
    return result.astype(jnp.bfloat16)


def solution(mesh):
    in_specs = (
        P("aux", "basis", None, None),
        P("aux", "basis", None),
        P("aux", "basis"),
        P(None, "basis"),
        P("basis", "aux"),
    )
    out_specs = P(("aux", "basis"), None)
    return jax.shard_map(local, mesh=mesh, in_specs=in_specs, out_specs=out_specs, check_vma=False)
```

profile of v0, /device:TPU:0, one launch (start us, length us, event | category | flops | bytes accessed | tf_op | source)
XLA Modules:
  0.0 162.2 jit_solution(17265205325925403429)
XLA Ops:
  6.5 0.0 all-gather.2.cloned.1.call-start
  6.5 0.8 fusion.20
  7.3 1.7 %collective-permute-start = (bf16[8,1024]{1,0:T(8,128)(2,1)S(1)}, bf16[8,1024]{1,0:T(8,128)(2,1)S(1)}, u32[]{:S(2)}, u32[]{:S(2)}) collective-permute-start(bf16[8,1024]{1,0:T(8,128)(2,1)S(1)} %get-tuple-element.7), channel_id=1, source_target_pairs={{0,1},{1,2},{2,3},{3,4},{4,5},{5,6},{6,7},{7,8},{8,9},{9,10},{10,1... | collective-permute-start | bytes 49160 | tf_op jit(solution)/shard_map/ppermute | solution.py:20
  9.0 4.9 %collective-permute-start.1 = (bf16[8,1024]{1,0:T(8,128)(2,1)S(1)}, bf16[8,1024]{1,0:T(8,128)(2,1)S(1)}, u32[]{:S(2)}, u32[]{:S(2)}) collective-permute-start(bf16[8,1024]{1,0:T(8,128)(2,1)S(1)} %get-tuple-element.8), channel_id=1, source_target_pairs={{1,0},{2,1},{3,2},{4,3},{5,4},{6,5},{7,6},{8,7},{9,8},{10,9},{11,1... | collective-permute-start | bytes 49160 | tf_op jit(solution)/shard_map/ppermute | solution.py:21
  13.9 0.7 subtract_bitcast_fusion
  14.6 0.7 compare_and_fusion
  16.0 0.0 collective-permute-done
  16.0 0.0 collective-permute-done.1
  16.0 0.8 maximum_bitcast_fusion
  16.8 0.6 gather_fusion
  17.4 6.4 %fusion = f32[48,8,8,128]{3,1,2,0:T(8,128)S(1)} fusion(bf16[8,48,128,128]{3,2,1,0:T(8,128)(2,1)} %param.5, bf16[48,8,128]{2,1,0:T(8,128)(2,1)S(1)} %gather_fusion, pred[48]{0:T(512)(128)(4,1)S(1)} %get-tuple-element.5), kind=kOutput, calls=%fused_computation.1 | convolution fusion | flops 100712448 | bytes 14254128 | tf_op jit(solution)/shard_map/qkmn,ikn->qikm/dot_general | solution.py:37
  23.8 1.6 fusion.7
  25.4 0.8 copy.24
  26.1 0.0 all-gather.2.cloned.1.call-update
  26.1 0.0 reduce-scatter.2.cloned.1.call-start
  26.2 25.8 %all-gather.2.cloned.1.call-done = bf16[512,1920]{1,0:T(8,128)(2,1)} async-done(((bf16[64,1920]{1,0:T(8,128)(2,1)}), bf16[512,1920]{1,0:T(8,128)(2,1)}) %all-gather.2.cloned.1.call-update) | async-done | bytes 1966096 | tf_op jit(solution)/shard_map/all_gather | solution.py:44
  52.0 14.8 %convolution_bitcast_fusion = f32[4096,512]{0,1:T(8,128)} fusion(bf16[512,1920]{1,0:T(8,128)(2,1)} %all-gather.2.cloned.1.call-done, bf16[1920,4096]{1,0:T(8,128)(2,1)} %param.9), kind=kOutput, calls=%fused_computation.3 | convolution fusion | flops 8053063680 | bytes 26083328 | tf_op jit(solution)/shard_map/dot_general | solution.py:46
  66.9 0.0 reduce-scatter.2.cloned.1.call-update
  66.9 86.5 %reduce-scatter.2.cloned.1.call-done = f32[256,512]{0,1:T(8,128)} async-done(((f32[4096,512]{0,1:T(8,128)}), f32[256,512]{0,1:T(8,128)}) %reduce-scatter.2.cloned.1.call-update) | async-done | bytes 524304 | tf_op jit(solution)/shard_map/reduce_scatter | solution.py:45
  153.4 1.1 convert_element_type.24
  154.5 0.8 copy.7
  (3 shorter events, 0.0 us)
Async XLA Ops:
  6.5 45.5 %all-gather.2.cloned.1.call-start = ((), (), s32[]{:S(2)}) async-start(), calls=%async_computation.1 | async-start | bytes 2211840 | tf_op jit(solution)/shard_map/all_gather | solution.py:44
  7.3 8.7 %collective-permute-start = (bf16[8,1024]{1,0:T(8,128)(2,1)S(1)}, bf16[8,1024]{1,0:T(8,128)(2,1)S(1)}, u32[]{:S(2)}, u32[]{:S(2)}) collective-permute-start(bf16[8,1024]{1,0:T(8,128)(2,1)S(1)} %get-tuple-element.7), channel_id=1, source_target_pairs={{0,1},{1,2},{2,3},{3,4},{4,5},{5,6},{6,7},{7,8},{8,9},{9,10},{10,1... | collective-permute-start | bytes 49160 | tf_op jit(solution)/shard_map/ppermute | solution.py:20
  9.0 7.0 %collective-permute-start.1 = (bf16[8,1024]{1,0:T(8,128)(2,1)S(1)}, bf16[8,1024]{1,0:T(8,128)(2,1)S(1)}, u32[]{:S(2)}, u32[]{:S(2)}) collective-permute-start(bf16[8,1024]{1,0:T(8,128)(2,1)S(1)} %get-tuple-element.8), channel_id=1, source_target_pairs={{1,0},{2,1},{3,2},{4,3},{5,4},{6,5},{7,6},{8,7},{9,8},{10,9},{11,1... | collective-permute-start | bytes 49160 | tf_op jit(solution)/shard_map/ppermute | solution.py:21
  26.1 127.3 %reduce-scatter.2.cloned.1.call-start = ((), (), s32[]{:S(2)}) async-start(), calls=%async_computation.2 | async-start | bytes 8912896 | tf_op jit(solution)/shard_map/reduce_scatter | solution.py:45
Sparse Core Ops, SparseCore 0:
  26.3 25.7 all-gather.1
  67.0 86.3 reduce-scatter.1
where the time goes:
time: 162 us
  waiting for transfers between devices  112 us (69%)
  matrix products  22.8 us (14%)
  between operations  14.1 us (9%)
  starting transfers between devices  6.65 us (4%)
  other arithmetic  3.22 us (2%)
  local copies, waits for them, and re-layouts  3.01 us (2%)
    reduce_scatter x1, waiting for transfers between devices, local(): lax.psum_scatter(lax.dot_general(virt_coef, gathered, (((0,), (1,)), ((),...  86.5 us
    all_gather x1, waiting for transfers between devices, local(): gathered = lax.all_gather(half_rows, 'aux', axis=0, tiled=True)  25.8 us
    dot_general x1, matrix products, local(): lax.dot_general(virt_coef, gathered, (((0,), (1,)), ((), ())), preferred_...  14.8 us
    dot_general x1, matrix products, local(): jnp.einsum('qkmn,ikn->qikm', v_blocks, picked, preferred_element_type=jnp...  6.39 us
    ppermute x1, starting transfers between devices, extended(): after = lax.ppermute(initial, axis, down)  4.91 us
  transfers between devices with their start and end apart: 4, of which 2 were waited for; matrix products, arithmetic and copies ran while one was open for 1% of the time, Pallas kernels for 0%

commit v1 on v0

v1 whole, which is shorter than its diff:
```python
import functools

import jax
import jax.numpy as jnp
from jax import lax
from jax.experimental import pallas as pl
from jax.experimental.pallas import tpu as pltpu
from jax.sharding import PartitionSpec as P

BB = 128
NOCC = 8
NEAR = 8
PAIR_CAP = 48
NB = 240
Q = 8
HERE = 15
ROWS = HERE * BB
COLS = 4096
TILE = 256
SIDE = 4
PIECES = 4
GROUPS = ((0, 128), (128, 256), (384, 128))
MESH = pl.DeviceIdType.MESH
F32 = jnp.float32
BF16 = jnp.bfloat16


def kernel(
    pm,
    pc,
    v_hbm,
    occ_hbm,
    virt_hbm,
    out_ref,
    v,
    virt,
    occ,
    halo,
    tab,
    lhs,
    hall,
    part,
    rel1,
    in1,
    tsum,
    own,
    rel2,
    in2,
    vsem,
    wsem,
    osem,
    hs,
    hr,
    gs,
    gr,
    ss,
    sr,
):
    aux = lax.axis_index("aux")
    basis = lax.axis_index("basis")
    x, c = aux // 2, aux % 2
    z, y = basis // SIDE, basis % SIDE

    partner = (2 * x + 1 - c, basis)
    x_up = (2 * ((x + 1) % SIDE) + c, basis)
    x_down = (2 * ((x + 3) % SIDE) + c, basis)
    y_up = (aux, z * SIDE + (y + 1) % SIDE)
    y_down = (aux, z * SIDE + (y + 3) % SIDE)
    z_up = (aux, ((z + 1) % SIDE) * SIDE + y)
    z_down = (aux, ((z + 3) % SIDE) * SIDE + y)
    b_up = (aux, (basis + 1) % (SIDE * SIDE))
    b_down = (aux, (basis + SIDE * SIDE - 1) % (SIDE * SIDE))

    def remote(src, dst, send, recv, peer):
        return pltpu.make_async_remote_copy(
            src_ref=src,
            dst_ref=dst,
            send_sem=send,
            recv_sem=recv,
            device_id={"aux": peer[0], "basis": peer[1]},
            device_id_type=MESH,
        )

    v_copies = [
        pltpu.make_async_copy(v_hbm.at[pl.ds(2 * p, 2)], v.at[pl.ds(2 * p, 2)], vsem.at[p])
        for p in range(PIECES)
    ]
    occ_copy = pltpu.make_async_copy(occ_hbm, occ, osem)
    occ_copy.start()
    for copy in v_copies:
        copy.start()

    barrier = pltpu.get_barrier_semaphore()
    peers = (partner, x_up, x_down, y_up, y_down, z_up, z_down, b_up, b_down)
    for peer in peers:
        pl.semaphore_signal(
            barrier, inc=1, device_id={"aux": peer[0], "basis": peer[1]}, device_id_type=MESH
        )
    pl.semaphore_wait(barrier, len(peers))

    started = []

    def go(copy):
        copy.start()
        started.append(copy)

    width = NEAR * BB
    to_up = remote(occ_hbm.at[:, pl.ds(ROWS - width, width)], halo.at[0], hs.at[0], hr.at[0], b_up)
    to_down = remote(occ_hbm.at[:, pl.ds(0, width)], halo.at[1], hs.at[1], hr.at[1], b_down)
    go(to_up)
    go(to_down)
    virt_copies = [
        pltpu.make_async_copy(
            virt_hbm.at[:, pl.ds(j * 1024, 1024)], virt.at[:, pl.ds(j * 1024, 1024)], wsem.at[j]
        )
        for j in range(SIDE)
    ]
    occ_copy.wait()
    for j in range(HERE):
        tab[NEAR + j] = occ[:, j * BB : (j + 1) * BB].astype(F32)
    to_up.wait_recv()
    to_down.wait_recv()
    for copy in virt_copies:
        copy.start()
    for j in range(NEAR):
        tab[j] = halo[0, :, j * BB : (j + 1) * BB].astype(F32)
        tab[NEAR + HERE + j] = halo[1, :, j * BB : (j + 1) * BB].astype(F32)

    first = basis * HERE
    row_block = lax.broadcasted_iota(jnp.int32, (BB, BB), 0) // NOCC

    def build(k, _):
        mu = pm[0, k, 0]
        nu = pm[0, k, 1]
        place = jnp.where(k < pc[0, 0], mu - first, -1)
        pos = jnp.clip(lax.rem(nu - first + NEAR + NB, NB), 0, HERE + 2 * NEAR - 1)
        picked = tab[pos]
        stack = jnp.concatenate([picked] * (BB // NOCC), axis=0)
        lhs[:, pl.ds(pl.multiple_of(k * BB, BB), BB)] = jnp.where(
            row_block == place, stack, 0.0
        ).astype(BF16)
        return 0

    lax.fori_loop(0, PAIR_CAP, build, 0)

    def piece_row(position, core, p):
        return pl.multiple_of(position * 128 + core * 64 + p * 16, 16)

    def rows16(row):
        return hall.at[pl.ds(row, 16)]

    def gather(message, p, position_src, position_dst, core, peer):
        return remote(
            rows16(piece_row(position_src, core, p)),
            rows16(piece_row(position_dst, core, p)),
            gs.at[message, p],
            gr.at[message, p],
            peer,
        )

    def arrived(message, p, position, core, peer):
        ref = rows16(piece_row(position, core, p))
        remote(ref, ref, gs.at[message, p], gr.at[message, p], peer).wait_recv()

    for p in range(PIECES):
        v_copies[p].wait()
        acc = jnp.zeros((BB, 2 * BB), F32)
        for k in range(0, PAIR_CAP, 2):
            w = jnp.concatenate(
                [
                    jnp.concatenate([v[2 * p + e, k], v[2 * p + e, k + 1]], axis=1)
                    for e in range(2)
                ],
                axis=0,
            )
            acc += lax.dot_general(
                lhs[:, k * BB : (k + 2) * BB],
                w,
                (((1,), (1,)), ((), ())),
                preferred_element_type=F32,
            )
        row = piece_row(0, c, p)
        for j in range(HERE):
            lines = acc[j * NOCC : (j + 1) * NOCC]
            both = jnp.concatenate([lines[:, :BB], lines[:, BB:]], axis=0)
            hall[pl.ds(row, 16), j * BB : (j + 1) * BB] = both.astype(BF16)
        go(gather(0, p, 0, 0, c, partner))
        go(gather(1, p, 0, 2, c, x_up))
        go(gather(2, p, 0, 1, c, x_down))

    relay_peer = (2 * ((x + 1 + 2 * c) % SIDE) + c, basis)

    def forward_near():
        for p in range(PIECES):
            arrived(1, p, 2, c, x_down)
            go(gather(3, p, 2, 2, c, partner))
            arrived(2, p, 1, c, x_up)
            go(gather(4, p, 1, 1, c, partner))
            go(gather(5, p, 2 - c, 3, c, relay_peer))

    def forward_far():
        for p in range(PIECES):
            arrived(5, p, 3, c, relay_peer)
            go(gather(6, p, 3, 3, c, partner))

    def chunk(g, zt, yt):
        r0, rows = GROUPS[g]
        column = pl.multiple_of((zt * SIDE + yt) * TILE, TILE)
        acc = jnp.dot(
            hall[pl.ds(r0, rows), :], virt[:, pl.ds(column, TILE)], preferred_element_type=F32
        )
        part[zt, yt, pl.ds(r0, rows), :] = acc.astype(BF16)

    def at(here, delta):
        return (here + delta) % SIDE

    def segment(g, fixed, delta, count, start):
        def body(i, _):
            other = i + start
            if fixed == "y":
                chunk(g, at(z, other), at(y, delta))
            else:
                chunk(g, at(z, delta), at(y, other))
            return 0

        lax.fori_loop(0, count, body, 0)

    def lines(g, half, which):
        r0, rows = GROUPS[g]
        quarter = rows // 4
        return (
            pl.ds(r0 + half * 2 * quarter + which * quarter, quarter),
            pl.ds(r0 // 2 + which * quarter, quarter),
            pl.ds(r0 // 4, quarter),
        )

    def ring(half, phase):
        along_y = half == phase
        return (y, y_up, y_down) if along_y else (z, z_up, z_down)

    def messages(g, half, phase):
        here, up, down = ring(half, phase)

        def source(target, which):
            hall_rows, half_rows, _ = lines(g, half, which)
            if phase == 1:
                return tsum.at[half, target, half_rows, :]
            if half == 0:
                return part.at[:, target, hall_rows, :]
            return part.at[target, :, hall_rows, :]

        def relay(direction):
            rows = lines(g, half, 0)[2]
            if phase == 1:
                return rel2.at[half, direction, rows, :]
            return rel1.at[half, direction, :, rows, :]

        def landing(direction, which):
            rows = lines(g, half, which)[1]
            if phase == 1:
                return in2.at[half, direction, rows, :]
            return in1.at[half, direction, :, rows, :]

        def make(j, src, dst, peer):
            return remote(src, dst, ss.at[g, half, phase, j], sr.at[g, half, phase, j], peer)

        return (
            make(0, source(at(here, 2), 0), relay(0), up),
            make(1, source(at(here, 2), 1), relay(1), down),
            make(2, source(at(here, 1), 1), landing(0, 1), up),
            make(3, source(at(here, 1), 0), landing(0, 0), up),
            make(4, source(at(here, 3), 0), landing(1, 0), down),
            make(5, source(at(here, 3), 1), landing(1, 1), down),
        )

    everything = {
        (g, half, phase): messages(g, half, phase)
        for g in range(len(GROUPS))
        for half in range(2)
        for phase in range(2)
    }

    def send(g, half, phase, *which):
        for j in which:
            go(everything[g, half, phase][j])

    def wait(g, half, phase, *which):
        for j in which:
            everything[g, half, phase][j].wait_recv()

    def relay1(g, half):
        here = ring(half, 0)[0]
        for direction, arrival, onward, delta, which in ((0, 0, 3, 1, 0), (1, 1, 5, 3, 1)):
            wait(g, half, 0, arrival)
            hall_rows, _, quarter = lines(g, half, which)
            target = at(here, delta)

            def body(t, _):
                zt, yt = (t, target) if half == 0 else (target, t)
                total = part[zt, yt, hall_rows, :].astype(F32) + rel1[
                    half, direction, t, quarter, :
                ].astype(F32)
                part[zt, yt, hall_rows, :] = total.astype(BF16)
                return 0

            lax.fori_loop(0, SIDE, body, 0)
            send(g, half, 0, onward)

    def middle(g, half):
        wait(g, half, 0, 2, 3, 4, 5)
        r0, rows = GROUPS[g]
        count = rows // 2
        hall_rows = pl.ds(r0 + half * count, count)
        half_rows = pl.ds(r0 // 2, count)
        other = z if half == 0 else y

        def total(delta):
            t = at(other, delta)
            zt, yt = (t, y) if half == 0 else (z, t)
            return t, (
                part[zt, yt, hall_rows, :].astype(F32)
                + in1[half, 0, t, half_rows, :].astype(F32)
                + in1[half, 1, t, half_rows, :].astype(F32)
            )

        for delta, sends in ((2, (0, 1)), (1, (2,)), (3, (4,))):
            t, value = total(delta)
            tsum[half, t, half_rows, :] = value.astype(BF16)
            send(g, half, 1, *sends)
        own[half, half_rows, :] = total(0)[1]

    def relay2(g, half):
        other = z if half == 0 else y
        for direction, arrival, onward, delta, which in ((0, 0, 3, 1, 0), (1, 1, 5, 3, 1)):
            wait(g, half, 1, arrival)
            _, half_rows, quarter = lines(g, half, which)
            target = at(other, delta)
            value = tsum[half, target, half_rows, :].astype(F32) + rel2[
                half, direction, quarter, :
            ].astype(F32)
            tsum[half, target, half_rows, :] = value.astype(BF16)
            send(g, half, 1, onward)

    def finish(g):
        r0, rows = GROUPS[g]
        count = rows // 2
        half_rows = pl.ds(r0 // 2, count)
        totals = []
        for half in range(2):
            wait(g, half, 1, 2, 3, 4, 5)
            totals.append(
                own[half, half_rows, :]
                + in2[half, 0, half_rows, :].astype(F32)
                + in2[half, 1, half_rows, :].astype(F32)
            )
        value = jnp.concatenate(totals, axis=0)
        for position in range(r0 // 128, (r0 + rows) // 128):
            chip = (x + (0, 1, 3, 2)[position]) % SIDE
            block = value[position * 128 - r0 : position * 128 - r0 + 128]
            out_ref[:, pl.ds(pl.multiple_of(chip * 128, 128), 128)] = block.T.astype(BF16)

    def compute(g, between):
        segment(g, "y", 2, 4, 2)
        send(g, 0, 0, 0, 1)
        segment(g, "z", 2, 3, 3)
        send(g, 1, 0, 0, 1)
        between()
        segment(g, "y", 1, 3, 3)
        send(g, 0, 0, 2)
        segment(g, "y", 3, 3, 3)
        send(g, 0, 0, 4)
        segment(g, "y", 0, 3, 3)
        send(g, 1, 0, 2, 4)
        for half in range(2):
            relay1(g, half)

    for p in range(PIECES):
        arrived(0, p, 0, 1 - c, partner)
    for copy in virt_copies:
        copy.wait()

    compute(0, forward_near)

    for p in range(PIECES):
        arrived(3, p, 2, 1 - c, partner)
        arrived(4, p, 1, 1 - c, partner)

    def between1():
        forward_far()
        middle(0, 0)
        middle(0, 1)

    compute(1, between1)
    relay2(0, 0)
    relay2(0, 1)
    for p in range(PIECES):
        arrived(6, p, 3, 1 - c, partner)

    def between2():
        middle(1, 0)
        middle(1, 1)

    compute(2, between2)
    relay2(1, 0)
    relay2(1, 1)
    finish(0)
    middle(2, 0)
    middle(2, 1)
    finish(1)
    relay2(2, 0)
    relay2(2, 1)
    finish(2)
    for copy in started:
        copy.wait_send()


def local(v_blocks, pair_map, pair_count, occ_coef, virt_coef):
    anywhere = pl.BlockSpec(memory_space=pl.ANY)
    scalars = pl.BlockSpec(memory_space=pltpu.SMEM)
    groups = len(GROUPS)
    return pl.pallas_call(
        kernel,
        out_shape=jax.ShapeDtypeStruct((TILE, 512), BF16),
        in_specs=[scalars, scalars, anywhere, anywhere, anywhere],
        out_specs=pl.BlockSpec(memory_space=pltpu.VMEM),
        scratch_shapes=[
            pltpu.VMEM((Q, PAIR_CAP, BB, BB), BF16),
            pltpu.VMEM((ROWS, COLS), BF16),
            pltpu.VMEM((NOCC, ROWS), BF16),
            pltpu.VMEM((2, NOCC, NEAR * BB), BF16),
            pltpu.VMEM((HERE + 2 * NEAR, NOCC, BB), F32),
            pltpu.VMEM((BB, PAIR_CAP * BB), BF16),
            pltpu.VMEM((512, ROWS), BF16),
            pltpu.VMEM((SIDE, SIDE, 512, TILE), BF16),
            pltpu.VMEM((2, 2, SIDE, 128, TILE), BF16),
            pltpu.VMEM((2, 2, SIDE, 256, TILE), BF16),
            pltpu.VMEM((2, SIDE, 256, TILE), BF16),
            pltpu.VMEM((2, 256, TILE), F32),
            pltpu.VMEM((2, 2, 128, TILE), BF16),
            pltpu.VMEM((2, 2, 256, TILE), BF16),
            pltpu.SemaphoreType.DMA((PIECES,)),
            pltpu.SemaphoreType.DMA((SIDE,)),
            pltpu.SemaphoreType.DMA,
            pltpu.SemaphoreType.DMA((2,)),
            pltpu.SemaphoreType.DMA((2,)),
            pltpu.SemaphoreType.DMA((7, PIECES)),
            pltpu.SemaphoreType.DMA((7, PIECES)),
            pltpu.SemaphoreType.DMA((groups, 2, 2, 6)),
            pltpu.SemaphoreType.DMA((groups, 2, 2, 6)),
        ],
        compiler_params=pltpu.CompilerParams(
            collective_id=0, has_side_effects=True, vmem_limit_bytes=60 << 20
        ),
        name="occupied_batch",
    )(pair_map, pair_count, v_blocks, occ_coef, virt_coef)


def solution(mesh):
    in_specs = (
        P("aux", "basis", None, None),
        P("aux", "basis", None),
        P("aux", "basis"),
        P(None, "basis"),
        P("basis", "aux"),
    )
    out_specs = P(("aux", "basis"), None)
    return jax.shard_map(local, mesh=mesh, in_specs=in_specs, out_specs=out_specs, check_vma=False)
```

time: 162 us -> 66.6 us (0.41)
  waiting for transfers between devices: 112 us -> 0 us
  Pallas kernels: 0 us -> 61.8 us
  matrix products: 22.8 us -> 0 us
  between operations: 14.1 us -> 0.66 us
  starting transfers between devices: 6.65 us -> 0 us
  other arithmetic: 3.22 us -> 0 us
    reduce_scatter x1 -> x0, waiting for transfers between devices: 86.5 us -> none  [local(): lax.psum_scatter(lax.dot_general(virt_coef, gathered, (((0,), (1,)), ((),...]
    pallas_call x0 -> x1, Pallas kernels: none -> 61.8 us  [local(): pl.pallas_call(kernel, out_shape=jax.ShapeDtypeStruct((TILE, 512), BF16),...]
    all_gather x1 -> x0, waiting for transfers between devices: 25.8 us -> none  [local(): gathered = lax.all_gather(half_rows, 'aux', axis=0, tiled=True)]
    dot_general x3 -> x0, matrix products: 22.8 us -> none  [the longest x1 14.8 us: local(): lax.dot_general(virt_coef, gathered, (((0,), (1,)), ((), ())), preferred_...]
    ppermute x2 -> x0, starting transfers between devices: 6.6 us -> none  [the longest x1 4.91 us: extended(): after = lax.ppermute(initial, axis, down)]
    unnamed x1 -> x2, local copies, waits for them, and re-layouts: 0.76 us -> 3.04 us
  transfers between devices with their start and end apart: 4 -> 0, of which waited for: 2 -> 0; matrix products, arithmetic and copies ran while one was open for 1% -> 0% of each run, Pallas kernels for 0% -> 0%
where the time goes in v1:
time: 66.6 us; the launch traced here: 65.5 us
  Pallas kernels  61.8 us (93%)
  local copies, waits for them, and re-layouts  3.04 us (5%)
    pallas_call x1, Pallas kernels, local(): pl.pallas_call(kernel, out_shape=jax.ShapeDtypeStruct((TILE, 512), BF16),...  61.8 us
    unnamed x2, local copies, waits for them, and re-layouts  3.04 us

profile of v1, /device:TPU:0, one launch (start us, length us, event | category | flops | bytes accessed | tf_op | source)
XLA Modules:
  0.0 65.5 jit_solution(14543580103872512699)
XLA Ops:
  0.7 1.4 %copy.6.pm = s32[1,48,2]{2,1,0:T(8,128)} copy(s32[1,48,2]{1,2,0:T(2,128)} %param.6) | data formatting | bytes 768 | tf_op args[1]
  2.0 61.8 %occupied_batch.1 = bf16[256,512]{1,0:T(8,128)(2,1)} custom-call(s32[1,48,2]{2,1,0:T(8,128)} %copy.6.pm, s32[1,1]{1,0:T(1,128)S(6)} %copy.8.pc, bf16[8,48,128,128]{3,2,1,0:T(8,128)(2,1)} %v_hbm.1, bf16[8,1920]{1,0:T(8,128)(2,1)} %occ_hbm.1, bf16[1920,4096]{1,0:T(8,128)(2,1)} %virt_hbm.1), custom_call_target="tpu_custom_call" | custom-call | tf_op jit(solution)/shard_map/occupied_batch/pallas_call | solution.py:421
  63.8 1.7 %copy.9 = bf16[256,512]{1,0:T(8,128)(2,1)} copy(bf16[256,512]{1,0:T(8,128)(2,1)} %occupied_batch.1) | data formatting | bytes 524288

commit v2 on v0

v2 whole, which is shorter than its diff:
```python
import functools

import jax
import jax.numpy as jnp
from jax import lax
from jax.experimental import pallas as pl
from jax.experimental.pallas import tpu as pltpu
from jax.sharding import PartitionSpec as P

BB = 128
NOCC = 8
NEAR = 8
PAIR_CAP = 48
NB = 240
Q = 8
HERE = 15
ROWS = HERE * BB
COLS = 4096
TILE = 256
SIDE = 4
PIECES = 4
GROUPS = ((0, 128), (128, 384))
ORDER = (
    (2, 2), (1, 2), (2, 1), (3, 2), (2, 3), (0, 2), (2, 0), (1, 1),
    (3, 1), (1, 3), (3, 3), (0, 1), (1, 0), (0, 3), (3, 0), (0, 0),
)
MESH = pl.DeviceIdType.MESH
F32 = jnp.float32
BF16 = jnp.bfloat16


def kernel(
    pm_hbm,
    pc_hbm,
    v_hbm,
    occ_hbm,
    virt_hbm,
    out_ref,
    pm,
    pc,
    v,
    virt,
    occ,
    halo,
    tab,
    lhs,
    hall,
    part,
    rel1,
    in1,
    tsum,
    own,
    rel2,
    in2,
    isem,
    vsem,
    wsem,
    sends,
    hr,
    gr,
    gr_all,
    r1,
    l1,
    r2,
    l2,
):
    aux = lax.axis_index("aux")
    basis = lax.axis_index("basis")
    x, c = aux // 2, aux % 2
    z, y = basis // SIDE, basis % SIDE

    partner = (2 * x + 1 - c, basis)
    x_up = (2 * ((x + 1) % SIDE) + c, basis)
    x_down = (2 * ((x + 3) % SIDE) + c, basis)
    y_up = (aux, z * SIDE + (y + 1) % SIDE)
    y_down = (aux, z * SIDE + (y + 3) % SIDE)
    z_up = (aux, ((z + 1) % SIDE) * SIDE + y)
    z_down = (aux, ((z + 3) % SIDE) * SIDE + y)
    b_up = (aux, (basis + 1) % (SIDE * SIDE))
    b_down = (aux, (basis + SIDE * SIDE - 1) % (SIDE * SIDE))
    x_relay = (2 * ((x + 1 + 2 * c) % SIDE) + c, basis)

    barrier = pltpu.get_barrier_semaphore()
    peers = (b_up, b_down, z_up, z_down, y_up, y_down, x_up, x_down, partner)
    for peer in peers:
        pl.semaphore_signal(
            barrier, inc=1, device_id={"aux": peer[0], "basis": peer[1]}, device_id_type=MESH
        )

    def remote(src, dst, send, recv, peer):
        return pltpu.make_async_remote_copy(
            src_ref=src,
            dst_ref=dst,
            send_sem=send,
            recv_sem=recv,
            device_id={"aux": peer[0], "basis": peer[1]},
            device_id_type=MESH,
        )

    small = (
        pltpu.make_async_copy(occ_hbm, occ, isem.at[0]),
        pltpu.make_async_copy(pm_hbm, pm, isem.at[1]),
        pltpu.make_async_copy(pc_hbm, pc, isem.at[2]),
    )
    for copy in small:
        copy.start()

    def v_copy(p):
        return pltpu.make_async_copy(v_hbm.at[pl.ds(2 * p, 2)], v.at[pl.ds(2 * p, 2)], vsem.at[p])

    for p in range(PIECES):
        v_copy(p).start()
    virt_copies = [
        pltpu.make_async_copy(
            virt_hbm.at[:, pl.ds(j * 1024, 1024)], virt.at[:, pl.ds(j * 1024, 1024)], wsem.at[j]
        )
        for j in range(SIDE)
    ]
    with jax.named_scope("t_barrier"):
        pl.semaphore_wait(barrier, len(peers))

    width = NEAR * BB
    small[0].wait()
    to_up = remote(occ.at[:, pl.ds(ROWS - width, width)], halo.at[0], sends.at[0], hr.at[0], b_up)
    to_down = remote(occ.at[:, pl.ds(0, width)], halo.at[1], sends.at[0], hr.at[1], b_down)
    to_up.start()
    to_down.start()
    for j in range(HERE):
        tab[NEAR + j] = occ[:, j * BB : (j + 1) * BB].astype(F32)
    small[1].wait()
    small[2].wait()
    with jax.named_scope("t_halo"):
        to_up.wait_recv()
        to_down.wait_recv()
    for copy in virt_copies:
        copy.start()
    for j in range(NEAR):
        tab[j] = halo[0, :, j * BB : (j + 1) * BB].astype(F32)
        tab[NEAR + HERE + j] = halo[1, :, j * BB : (j + 1) * BB].astype(F32)

    first = basis * HERE
    row_block = lax.broadcasted_iota(jnp.int32, (BB, BB), 0) // NOCC

    def build(k, _):
        mu = pm[0, 0, k]
        nu = pm[0, 1, k]
        place = jnp.where(k < pc[0, 0], mu - first, -1)
        pos = jnp.clip(lax.rem(nu - first + NEAR + NB, NB), 0, HERE + 2 * NEAR - 1)
        stack = jnp.concatenate([tab[pos]] * (BB // NOCC), axis=0)
        lhs[:, pl.ds(pl.multiple_of(k * BB, BB), BB)] = jnp.where(
            row_block == place, stack, 0.0
        ).astype(BF16)
        return 0

    with jax.named_scope("t_build"):
        lax.fori_loop(0, PAIR_CAP, build, 0, unroll=4)

    def piece_ref(position, core, p):
        return hall.at[pl.ds(pl.multiple_of(position * 128 + core * 64 + p * 16, 16), 16)]

    def gather_sem(message, p):
        if message in (1, 2, 5):
            return gr.at[(1, 2, 5).index(message), p]
        return gr_all.at[(0, 3, 4, 6).index(message)]

    def gather(message, p, position_src, position_dst, core, peer):
        return remote(
            piece_ref(position_src, core, p),
            piece_ref(position_dst, core, p),
            sends.at[1],
            gather_sem(message, p),
            peer,
        )

    def arrived(message, p, position, core, peer):
        ref = piece_ref(position, core, p)
        remote(ref, ref, sends.at[1], gather_sem(message, p), peer).wait_recv()

    def all_arrived(message, position):
        ref = hall.at[pl.ds(pl.multiple_of(position * 128 + (1 - c) * 64, 64), 64)]
        remote(ref, ref, sends.at[1], gather_sem(message, 0), partner).wait_recv()

    def first_half(p, _):
        v_copy(p).wait()
        acc = jnp.zeros((BB, 2 * BB), F32)
        for k in range(0, PAIR_CAP, 2):
            w = jnp.concatenate(
                [
                    jnp.concatenate([v[2 * p + e, k], v[2 * p + e, k + 1]], axis=1)
                    for e in range(2)
                ],
                axis=0,
            )
            acc += lax.dot_general(
                lhs[:, k * BB : (k + 2) * BB],
                w,
                (((1,), (1,)), ((), ())),
                preferred_element_type=F32,
            )
        row = pl.multiple_of(c * 64 + p * 16, 16)
        for j in range(HERE):
            lines = acc[j * NOCC : (j + 1) * NOCC]
            both = jnp.concatenate([lines[:, :BB], lines[:, BB:]], axis=0)
            hall[pl.ds(row, 16), j * BB : (j + 1) * BB] = both.astype(BF16)
        gather(0, p, 0, 0, c, partner).start()
        gather(1, p, 0, 2, c, x_up).start()
        gather(2, p, 0, 1, c, x_down).start()
        return 0

    with jax.named_scope("t_first"):
        lax.fori_loop(0, PIECES, first_half, 0)

    def forward_near(p, _):
        arrived(1, p, 2, c, x_down)
        gather(3, p, 2, 2, c, partner).start()
        arrived(2, p, 1, c, x_up)
        gather(4, p, 1, 1, c, partner).start()
        gather(5, p, 2 - c, 3, c, x_relay).start()
        return 0

    def forward_far(p, _):
        arrived(5, p, 3, c, x_relay)
        gather(6, p, 3, 3, c, partner).start()
        return 0

    def rows_of(g, half, which, count=1):
        r0, rows = GROUPS[g]
        quarter = rows // 4
        return (
            r0 + half * 2 * quarter + which * quarter,
            r0 // 2 + which * quarter,
            r0 // 4,
            quarter * count,
        )

    def ring(half, phase):
        return (y, y_up, y_down) if half == phase else (z, z_up, z_down)

    KINDS = ((0, 0, 0), (1, 1, 0), (1, 0, 1), (0, 0, 1), (0, 1, 1), (1, 1, 1))

    def message1(g, half, j, target, t):
        which, way, landing = KINDS[j]
        hall_row, half_row, quarter_row, n = rows_of(g, half, which)
        zt, yt = (t, target) if half == 0 else (target, t)
        if landing:
            dst = in1.at[half, way, t, pl.ds(half_row, n)]
        else:
            dst = rel1.at[half, way, t, pl.ds(quarter_row, n)]
        return remote(
            part.at[zt, yt, pl.ds(hall_row, n)],
            dst,
            sends.at[2],
            (l1 if landing else r1).at[g, half, t],
            ring(half, 0)[1 + way],
        )

    def neighbour1(g, half, way, target, t):
        hall_row, half_row, _, n = rows_of(g, half, 0)
        skip = (1 - way) * n
        zt, yt = (t, target) if half == 0 else (target, t)
        peer = (aux, z * SIDE + target) if half == 0 else (aux, target * SIDE + y)
        return remote(
            part.at[zt, yt, pl.ds(pl.multiple_of(hall_row + skip, 32), n)],
            in1.at[half, way, t, pl.ds(pl.multiple_of(half_row + skip, 32), n)],
            sends.at[2],
            l1.at[g, half, t],
            peer,
        )

    def message2(g, half, j, target):
        which, way, landing = KINDS[j]
        _, half_row, quarter_row, n = rows_of(g, half, which)
        if landing:
            dst = in2.at[half, way, pl.ds(half_row, n)]
        else:
            dst = rel2.at[half, way, pl.ds(quarter_row, n)]
        return remote(
            tsum.at[half, target, pl.ds(half_row, n)],
            dst,
            sends.at[3],
            (l2 if landing else r2).at[g, half],
            ring(half, 1)[1 + way],
        )

    def wait1(g, half, t, landing):
        _, half_row, quarter_row, n = rows_of(g, half, 0)
        if landing:
            ref, sem = in1.at[half, :, t, pl.ds(half_row, 2 * n)], l1.at[g, half, t]
        else:
            ref, sem = rel1.at[half, :, t, pl.ds(quarter_row, n)], r1.at[g, half, t]
        remote(ref, ref, sends.at[2], sem, ring(half, 0)[1]).wait_recv()

    def wait2(g, half, landing):
        _, half_row, quarter_row, n = rows_of(g, half, 0)
        if landing:
            ref, sem = in2.at[half, :, pl.ds(half_row, 2 * n)], l2.at[g, half]
        else:
            ref, sem = rel2.at[half, :, pl.ds(quarter_row, n)], r2.at[g, half]
        remote(ref, ref, sends.at[3], sem, ring(half, 1)[1]).wait_recv()

    def at(here, delta):
        return (here + delta) % SIDE

    def blocks(n, body):
        def step(i, _):
            body(i * 32)
            return 0

        lax.fori_loop(0, n // 32, step, 0)

    def rows32(start, i):
        return pl.ds(pl.multiple_of(start + i, 32), 32)

    def relay1(g, half, delta):
        here = ring(half, 0)[0]
        t = at(z if half == 0 else y, delta)
        wait1(g, half, t, False)
        for way, onward, step in ((0, 3, 1), (1, 5, 3)):
            target = at(here, step)
            zt, yt = (t, target) if half == 0 else (target, t)
            hall_row, _, quarter_row, n = rows_of(g, half, way)

            def body(i):
                total = part[zt, yt, rows32(hall_row, i), :].astype(F32) + rel1[
                    half, way, t, rows32(quarter_row, i), :
                ].astype(F32)
                part[zt, yt, rows32(hall_row, i), :] = total.astype(BF16)

            blocks(n, body)
            message1(g, half, onward, target, t).start()

    def middle(g, half, delta):
        t = at(z if half == 0 else y, delta)
        wait1(g, half, t, True)
        zt, yt = (t, y) if half == 0 else (z, t)
        hall_row, half_row, _, n = rows_of(g, half, 0, 2)

        def body(i):
            total = (
                part[zt, yt, rows32(hall_row, i), :].astype(F32)
                + in1[half, 0, t, rows32(half_row, i), :].astype(F32)
                + in1[half, 1, t, rows32(half_row, i), :].astype(F32)
            )
            if delta:
                tsum[half, t, rows32(half_row, i), :] = total.astype(BF16)
            else:
                own[half, rows32(half_row, i), :] = total

        blocks(n, body)
        for j in {0: (), 1: (2,), 2: (0, 1), 3: (4,)}[delta]:
            message2(g, half, j, t).start()

    def relay2(g, half):
        here = ring(half, 1)[0]
        wait2(g, half, False)
        for way, onward, step in ((0, 3, 1), (1, 5, 3)):
            target = at(here, step)
            _, half_row, quarter_row, n = rows_of(g, half, way)

            def body(i):
                total = tsum[half, target, rows32(half_row, i), :].astype(F32) + rel2[
                    half, way, rows32(quarter_row, i), :
                ].astype(F32)
                tsum[half, target, rows32(half_row, i), :] = total.astype(BF16)

            blocks(n, body)
            message2(g, half, onward, target).start()

    def finish(g, half):
        wait2(g, half, True)
        hall_row, half_row, _, n = rows_of(g, half, 0, 2)

        def body(i):
            rows = rows32(half_row, i)
            total = (
                own[half, rows, :]
                + in2[half, 0, rows, :].astype(F32)
                + in2[half, 1, rows, :].astype(F32)
            )
            row = hall_row + i
            position = row // 128
            chip = (x + position + position // 2 - 2 * (position // 3)) % SIDE
            out_ref[rows32(chip * 128, row % 128), :] = total.astype(BF16)

        blocks(n, body)

    def compute(g, services):
        r0, rows = GROUPS[g]

        def body(i, carry):
            deltas_y, deltas_z = carry
            dy, dz = deltas_y % SIDE, deltas_z % SIDE
            yt, zt = at(y, dy), at(z, dz)
            column = pl.multiple_of((zt * SIDE + yt) * TILE, TILE)
            acc = jnp.dot(
                hall[pl.ds(r0, rows), :], virt[:, pl.ds(column, TILE)], preferred_element_type=F32
            )
            part[zt, yt, pl.ds(r0, rows), :] = acc.astype(BF16)
            for half, d, target, t in ((0, dy, yt, zt), (1, dz, zt, yt)):

                @pl.when(d == 2)
                def _():
                    message1(g, half, 0, target, t).start()
                    message1(g, half, 1, target, t).start()

                @pl.when(d % 2 == 1)
                def _():
                    neighbour1(g, half, d // 2, target, t).start()

            @pl.when(i % 2 == 1)
            def _():
                services(i)

            return deltas_y // SIDE, deltas_z // SIDE

        lax.fori_loop(
            0,
            SIDE * SIDE,
            body,
            (
                jnp.int32(sum(d << (2 * i) for i, (d, _) in enumerate(ORDER))),
                jnp.int32(sum(d << (2 * i) for i, (_, d) in enumerate(ORDER))),
            ),
        )

    def both(function, g, *rest):
        for half in range(2):
            function(g, half, *rest)

    def loop(n, function):
        lax.fori_loop(0, n, function, 0)

    def scoped(name, function):
        def run():
            with jax.named_scope(name):
                function()

        return run

    def when(condition, name, function):
        pl.when(condition)(scoped(name, function))

    with jax.named_scope("t_part0"):
        all_arrived(0, 0)
    with jax.named_scope("t_virt"):
        for copy in virt_copies:
            copy.wait()

    def services0(i):
        when(i < 8, "t_near", lambda: forward_near(i // 2, 0))
        when(i == 13, "t_far", lambda: loop(PIECES, forward_far))

    with jax.named_scope("t_C0"):
        compute(0, services0)
    with jax.named_scope("t_relay0"):
        for delta in range(SIDE):
            both(relay1, 0, delta)
    with jax.named_scope("t_part1"):
        all_arrived(3, 2)
        all_arrived(4, 1)
        all_arrived(6, 3)

    def middle0():
        for delta in (2, 1, 3, 0):
            both(middle, 0, delta)

    def relays():
        for delta in (1, 3):
            both(relay1, 1, delta)

    def services1(i):
        when(i == 5, "t_mid0", middle0)
        when(i == 9, "t_rel2", lambda: both(relay1, 1, 2))
        when(i == 11, "t_relay20", lambda: both(relay2, 0))
        when(i == 13, "t_rel13", relays)
        when(i == 15, "t_mid2", lambda: both(middle, 1, 2))

    with jax.named_scope("t_C1"):
        compute(1, services1)
    with jax.named_scope("t_rel0"):
        both(relay1, 1, 0)
    with jax.named_scope("t_mid1"):
        both(middle, 1, 1)
    with jax.named_scope("t_mid3"):
        both(middle, 1, 3)
    with jax.named_scope("t_relay21"):
        both(relay2, 1)
    with jax.named_scope("t_fin0"):
        both(finish, 0)
    with jax.named_scope("t_midown"):
        both(middle, 1, 0)
    with jax.named_scope("t_fin1"):
        both(finish, 1)

    with jax.named_scope("t_sends"):
        for j, ref in enumerate(
            (halo, hall.at[pl.ds(0, 448)], part.at[pl.ds(0, 3)], part.at[0, pl.ds(0, 3)])
        ):
            remote(ref, ref, sends.at[j], hr.at[0], partner).wait_send()


def local(v_blocks, pair_map, pair_count, occ_coef, virt_coef):
    anywhere = pl.BlockSpec(memory_space=pl.ANY)
    groups = len(GROUPS)
    rows_first = pl.pallas_call(
        kernel,
        out_shape=jax.ShapeDtypeStruct((512, TILE), BF16),
        in_specs=[anywhere] * 5,
        out_specs=pl.BlockSpec(memory_space=pltpu.VMEM),
        scratch_shapes=[
            pltpu.SMEM((1, 2, PAIR_CAP), jnp.int32),
            pltpu.SMEM((1, 1), jnp.int32),
            pltpu.VMEM((Q, PAIR_CAP, BB, BB), BF16),
            pltpu.VMEM((ROWS, COLS), BF16),
            pltpu.VMEM((NOCC, ROWS), BF16),
            pltpu.VMEM((2, NOCC, NEAR * BB), BF16),
            pltpu.VMEM((HERE + 2 * NEAR, NOCC, BB), F32),
            pltpu.VMEM((BB, PAIR_CAP * BB), BF16),
            pltpu.VMEM((512, ROWS), BF16),
            pltpu.VMEM((SIDE, SIDE, 512, TILE), BF16),
            pltpu.VMEM((2, 2, SIDE, 128, TILE), BF16),
            pltpu.VMEM((2, 2, SIDE, 256, TILE), BF16),
            pltpu.VMEM((2, SIDE, 256, TILE), BF16),
            pltpu.VMEM((2, 256, TILE), F32),
            pltpu.VMEM((2, 2, 128, TILE), BF16),
            pltpu.VMEM((2, 2, 256, TILE), BF16),
            pltpu.SemaphoreType.DMA((3,)),
            pltpu.SemaphoreType.DMA((PIECES,)),
            pltpu.SemaphoreType.DMA((SIDE,)),
            pltpu.SemaphoreType.DMA((4,)),
            pltpu.SemaphoreType.DMA((2,)),
            pltpu.SemaphoreType.DMA((3, PIECES)),
            pltpu.SemaphoreType.DMA((4,)),
            pltpu.SemaphoreType.DMA((groups, 2, SIDE)),
            pltpu.SemaphoreType.DMA((groups, 2, SIDE)),
            pltpu.SemaphoreType.DMA((groups, 2)),
            pltpu.SemaphoreType.DMA((groups, 2)),
        ],
        compiler_params=pltpu.CompilerParams(
            collective_id=0, has_side_effects=True, vmem_limit_bytes=60 << 20
        ),
        name="occupied_batch",
    )(jnp.swapaxes(pair_map, 1, 2), pair_count, v_blocks, occ_coef, virt_coef)
    return rows_first.T


def solution(mesh):
    in_specs = (
        P("aux", "basis", None, None),
        P("aux", "basis", None),
        P("aux", "basis"),
        P(None, "basis"),
        P("basis", "aux"),
    )
    out_specs = P(("aux", "basis"), None)
    return jax.shard_map(local, mesh=mesh, in_specs=in_specs, out_specs=out_specs, check_vma=False)
```

time: 162 us -> 52 us (0.32)
  waiting for transfers between devices: 112 us -> 0 us
  Pallas kernels: 0 us -> 49.4 us
  matrix products: 22.8 us -> 0 us
  between operations: 14.1 us -> 0.66 us
  starting transfers between devices: 6.65 us -> 0 us
  other arithmetic: 3.22 us -> 0 us
    reduce_scatter x1 -> x0, waiting for transfers between devices: 86.5 us -> none  [local(): lax.psum_scatter(lax.dot_general(virt_coef, gathered, (((0,), (1,)), ((),...]
    pallas_call x0 -> x1, Pallas kernels: none -> 49.4 us  [local(): pl.pallas_call(kernel, out_shape=jax.ShapeDtypeStruct((512, TILE), BF16),...]
    all_gather x1 -> x0, waiting for transfers between devices: 25.8 us -> none  [local(): gathered = lax.all_gather(half_rows, 'aux', axis=0, tiled=True)]
    dot_general x3 -> x0, matrix products: 22.8 us -> none  [the longest x1 14.8 us: local(): lax.dot_general(virt_coef, gathered, (((0,), (1,)), ((), ())), preferred_...]
    ppermute x2 -> x0, starting transfers between devices: 6.6 us -> none  [the longest x1 4.91 us: extended(): after = lax.ppermute(initial, axis, down)]
    transpose x0 -> x1, local copies, waits for them, and re-layouts: none -> 1.8 us  [local(): return rows_first.T]
  transfers between devices with their start and end apart: 4 -> 0, of which waited for: 2 -> 0; matrix products, arithmetic and copies ran while one was open for 1% -> 0% of each run, Pallas kernels for 0% -> 0%
where the time goes in v2:
time: 52 us; the launch traced here: 51.8 us
  Pallas kernels  49.4 us (95%)
  local copies, waits for them, and re-layouts  1.8 us (3%)
  between operations  0.66 us (1%)
    pallas_call x1, Pallas kernels, local(): pl.pallas_call(kernel, out_shape=jax.ShapeDtypeStruct((512, TILE), BF16),...  49.4 us
    transpose x1, local copies, waits for them, and re-layouts, local(): return rows_first.T  1.8 us

profile of v2, /device:TPU:0, one launch (start us, length us, event | category | flops | bytes accessed | tf_op | source)
XLA Modules:
  0.0 51.8 jit_solution(13876546581686054383)
XLA Ops:
  0.7 49.4 %occupied_batch.1 = bf16[512,256]{1,0:T(8,128)(2,1)} custom-call(s32[1,2,48]{2,1,0:T(2,128)} %bitcast.3, s32[1,1]{1,0:T(1,128)S(6)} %copy.7.pc_hbm, bf16[8,48,128,128]{3,2,1,0:T(8,128)(2,1)} %v_hbm.1, bf16[8,1920]{1,0:T(8,128)(2,1)} %occ_hbm.1, bf16[1920,4096]{1,0:T(8,128)(2,1)} %virt_hbm.1), custom_call_target="tpu_custom_call" | custom-call | tf_op jit(solution)/shard_map/occupied_batch/pallas_call | solution.py:505
  50.0 1.8 %copy.6 = bf16[256,512]{1,0:T(8,128)(2,1)} copy(bf16[256,512]{0,1:T(8,128)(2,1)} %bitcast.2) | data formatting | bytes 524288 | tf_op jit(solution)/shard_map/transpose | solution.py:544

commit v3 on v2

--- a/solution.py
+++ b/solution.py
@@ -20,9 +20,13 @@
 SIDE = 4
 PIECES = 4
 GROUPS = ((0, 128), (128, 384))
-ORDER = (
-    (2, 2), (1, 2), (2, 1), (3, 2), (2, 3), (0, 2), (2, 0), (1, 1),
-    (3, 1), (1, 3), (3, 3), (0, 1), (1, 0), (0, 3), (3, 0), (0, 0),
+ORDER0 = (
+    (2, 2), (1, 2), (3, 2), (0, 2), (2, 1), (2, 3), (2, 0), (1, 1),
+    (3, 1), (0, 1), (1, 3), (3, 3), (0, 3), (1, 0), (3, 0), (0, 0),
+)
+ORDER1 = (
+    (2, 2), (1, 2), (2, 1), (3, 2), (2, 3), (1, 1), (3, 3), (1, 3),
+    (3, 1), (0, 2), (2, 0), (0, 1), (1, 0), (0, 3), (3, 0), (0, 0),
 )
 MESH = pl.DeviceIdType.MESH
 F32 = jnp.float32
@@ -35,6 +39,7 @@
     v_hbm,
     occ_hbm,
     virt_hbm,
+    out_hbm,
     out_ref,
     pm,
     pc,
@@ -46,7 +51,8 @@
     lhs,
     hall,
     part,
-    rel1,
+    rel0,
+    in0,
     in1,
     tsum,
     own,
@@ -59,10 +65,9 @@
     hr,
     gr,
     gr_all,
-    r1,
-    l1,
-    r2,
-    l2,
+    m0,
+    m1,
+    m2,
 ):
     aux = lax.axis_index("aux")
     basis = lax.axis_index("basis")
@@ -108,32 +113,34 @@
     def v_copy(p):
         return pltpu.make_async_copy(v_hbm.at[pl.ds(2 * p, 2)], v.at[pl.ds(2 * p, 2)], vsem.at[p])
 
+    def virt_copy(delta):
+        columns = pl.ds(pl.multiple_of((z + delta) % SIDE * 1024, 1024), 1024)
+        return pltpu.make_async_copy(
+            virt_hbm.at[:, columns], virt.at[:, columns], wsem.at[delta]
+        )
+
     for p in range(PIECES):
         v_copy(p).start()
-    virt_copies = [
-        pltpu.make_async_copy(
-            virt_hbm.at[:, pl.ds(j * 1024, 1024)], virt.at[:, pl.ds(j * 1024, 1024)], wsem.at[j]
-        )
-        for j in range(SIDE)
-    ]
+    for delta in (2, 1, 3, 0):
+        virt_copy(delta).start()
     with jax.named_scope("t_barrier"):
         pl.semaphore_wait(barrier, len(peers))
 
     width = NEAR * BB
-    small[0].wait()
+    with jax.named_scope("t_occ"):
+        small[0].wait()
     to_up = remote(occ.at[:, pl.ds(ROWS - width, width)], halo.at[0], sends.at[0], hr.at[0], b_up)
     to_down = remote(occ.at[:, pl.ds(0, width)], halo.at[1], sends.at[0], hr.at[1], b_down)
     to_up.start()
     to_down.start()
     for j in range(HERE):
         tab[NEAR + j] = occ[:, j * BB : (j + 1) * BB].astype(F32)
-    small[1].wait()
-    small[2].wait()
     with jax.named_scope("t_halo"):
         to_up.wait_recv()
         to_down.wait_recv()
-    for copy in virt_copies:
-        copy.start()
+    with jax.named_scope("t_small"):
+        small[1].wait()
+        small[2].wait()
     for j in range(NEAR):
         tab[j] = halo[0, :, j * BB : (j + 1) * BB].astype(F32)
         tab[NEAR + HERE + j] = halo[1, :, j * BB : (j + 1) * BB].astype(F32)
@@ -236,36 +243,45 @@
     def ring(half, phase):
         return (y, y_up, y_down) if half == phase else (z, z_up, z_down)
 
+    def at(here, delta):
+        return (here + delta) % SIDE
+
     KINDS = ((0, 0, 0), (1, 1, 0), (1, 0, 1), (0, 0, 1), (0, 1, 1), (1, 1, 1))
 
-    def message1(g, half, j, target, t):
+    def bulk(half, j, target):
         which, way, landing = KINDS[j]
-        hall_row, half_row, quarter_row, n = rows_of(g, half, which)
+        hall_row, half_row, quarter_row, n = rows_of(0, half, which)
+        rows = pl.ds(hall_row, n)
+        return remote(
+            part.at[:, target, rows] if half == 0 else part.at[target, :, rows],
+            in0.at[half, way, :, pl.ds(half_row, n)] if landing else rel0.at[half, way],
+            sends.at[2],
+            m0.at[landing, half],
+            ring(half, 0)[1 + way],
+        )
+
+    R0, RN = GROUPS[1]
+    QUARTER = RN // 4
+
+    def single(half, which, way, landing, target, t):
+        put = which * QUARTER if landing else 2 * QUARTER
         zt, yt = (t, target) if half == 0 else (target, t)
-        if landing:
-            dst = in1.at[half, way, t, pl.ds(half_row, n)]
-        else:
-            dst = rel1.at[half, way, t, pl.ds(quarter_row, n)]
         return remote(
-            part.at[zt, yt, pl.ds(hall_row, n)],
-            dst,
+            part.at[zt, yt, pl.ds(R0 + (2 * half + which) * QUARTER, QUARTER)],
+            in1.at[half, way, t, pl.ds(put, QUARTER)],
             sends.at[2],
-            (l1 if landing else r1).at[g, half, t],
+            m1.at[landing, half, t],
             ring(half, 0)[1 + way],
         )
 
-    def neighbour1(g, half, way, target, t):
-        hall_row, half_row, _, n = rows_of(g, half, 0)
-        skip = (1 - way) * n
-        zt, yt = (t, target) if half == 0 else (target, t)
-        peer = (aux, z * SIDE + target) if half == 0 else (aux, target * SIDE + y)
-        return remote(
-            part.at[zt, yt, pl.ds(pl.multiple_of(hall_row + skip, 32), n)],
-            in1.at[half, way, t, pl.ds(pl.multiple_of(half_row + skip, 32), n)],
-            sends.at[2],
-            l1.at[g, half, t],
-            peer,
-        )
+    def send_chunk(dy, dz):
+        yt, zt = at(y, dy), at(z, dz)
+        for half, d, target, t in ((0, dy, yt, zt), (1, dz, zt, yt)):
+            if d == 2:
+                single(half, 0, 0, 0, target, t).start()
+                single(half, 1, 1, 0, target, t).start()
+            elif d:
+                single(half, 1 - d // 2, d // 2, 1, target, t).start()
 
     def message2(g, half, j, target):
         which, way, landing = KINDS[j]
@@ -278,28 +294,26 @@
             tsum.at[half, target, pl.ds(half_row, n)],
             dst,
             sends.at[3],
-            (l2 if landing else r2).at[g, half],
+            m2.at[landing, g, half],
             ring(half, 1)[1 + way],
         )
 
-    def wait1(g, half, t, landing):
-        _, half_row, quarter_row, n = rows_of(g, half, 0)
-        if landing:
-            ref, sem = in1.at[half, :, t, pl.ds(half_row, 2 * n)], l1.at[g, half, t]
-        else:
-            ref, sem = rel1.at[half, :, t, pl.ds(quarter_row, n)], r1.at[g, half, t]
-        remote(ref, ref, sends.at[2], sem, ring(half, 0)[1]).wait_recv()
+    def wait1(half, t, landing):
+        rows = pl.ds(0, 2 * QUARTER) if landing else pl.ds(2 * QUARTER, QUARTER)
+        ref = in1.at[half, :, t, rows]
+        remote(ref, ref, sends.at[2], m1.at[landing, half, t], ring(half, 0)[1]).wait_recv()
+
+    def wait0(half, landing):
+        ref = in0.at[half] if landing else rel0.at[half]
+        remote(ref, ref, sends.at[2], m0.at[landing, half], ring(half, 0)[1]).wait_recv()
 
     def wait2(g, half, landing):
         _, half_row, quarter_row, n = rows_of(g, half, 0)
         if landing:
-            ref, sem = in2.at[half, :, pl.ds(half_row, 2 * n)], l2.at[g, half]
+            ref = in2.at[half, :, pl.ds(half_row, 2 * n)]
         else:
-            ref, sem = rel2.at[half, :, pl.ds(quarter_row, n)], r2.at[g, half]
-        remote(ref, ref, sends.at[3], sem, ring(half, 1)[1]).wait_recv()
-
-    def at(here, delta):
-        return (here + delta) % SIDE
+            ref = rel2.at[half, :, pl.ds(quarter_row, n)]
+        remote(ref, ref, sends.at[3], m2.at[landing, g, half], ring(half, 1)[1]).wait_recv()
 
     def blocks(n, body):
         def step(i, _):
@@ -311,35 +325,53 @@
     def rows32(start, i):
         return pl.ds(pl.multiple_of(start + i, 32), 32)
 
-    def relay1(g, half, delta):
+    def relay1(half, delta):
         here = ring(half, 0)[0]
         t = at(z if half == 0 else y, delta)
-        wait1(g, half, t, False)
+        wait1(half, t, 0)
+        for way, step in ((0, 1), (1, 3)):
+            target = at(here, step)
+            zt, yt = (t, target) if half == 0 else (target, t)
+            row = R0 + (2 * half + way) * QUARTER
+
+            def body(i):
+                total = part[zt, yt, rows32(row, i), :].astype(F32) + in1[
+                    half, way, t, rows32(2 * QUARTER, i), :
+                ].astype(F32)
+                part[zt, yt, rows32(row, i), :] = total.astype(BF16)
+
+            blocks(QUARTER, body)
+            single(half, way, way, 1, target, t).start()
+
+    def relay0(half):
+        here = ring(half, 0)[0]
+        wait0(half, 0)
         for way, onward, step in ((0, 3, 1), (1, 5, 3)):
             target = at(here, step)
-            zt, yt = (t, target) if half == 0 else (target, t)
-            hall_row, _, quarter_row, n = rows_of(g, half, way)
-
-            def body(i):
-                total = part[zt, yt, rows32(hall_row, i), :].astype(F32) + rel1[
-                    half, way, t, rows32(quarter_row, i), :
-                ].astype(F32)
-                part[zt, yt, rows32(hall_row, i), :] = total.astype(BF16)
-
-            blocks(n, body)
-            message1(g, half, onward, target, t).start()
+            row, _, _, n = rows_of(0, half, way)
+
+            def body(t, _):
+                zt, yt = (t, target) if half == 0 else (target, t)
+                total = part[zt, yt, pl.ds(row, n), :].astype(F32) + rel0[half, way, t].astype(F32)
+                part[zt, yt, pl.ds(row, n), :] = total.astype(BF16)
+                return 0
+
+            lax.fori_loop(0, SIDE, body, 0)
+            bulk(half, onward, target).start()
 
     def middle(g, half, delta):
         t = at(z if half == 0 else y, delta)
-        wait1(g, half, t, True)
+        if g:
+            wait1(half, t, 1)
         zt, yt = (t, y) if half == 0 else (z, t)
         hall_row, half_row, _, n = rows_of(g, half, 0, 2)
+        landed = in1 if g else in0
 
         def body(i):
             total = (
                 part[zt, yt, rows32(hall_row, i), :].astype(F32)
-                + in1[half, 0, t, rows32(half_row, i), :].astype(F32)
-                + in1[half, 1, t, rows32(half_row, i), :].astype(F32)
+                + landed[half, 0, t, rows32(0, i), :].astype(F32)
+                + landed[half, 1, t, rows32(0, i), :].astype(F32)
             )
             if delta:
                 tsum[half, t, rows32(half_row, i), :] = total.astype(BF16)
@@ -352,7 +384,7 @@
 
     def relay2(g, half):
         here = ring(half, 1)[0]
-        wait2(g, half, False)
+        wait2(g, half, 0)
         for way, onward, step in ((0, 3, 1), (1, 5, 3)):
             target = at(here, step)
             _, half_row, quarter_row, n = rows_of(g, half, way)
@@ -367,7 +399,7 @@
             message2(g, half, onward, target).start()
 
     def finish(g, half):
-        wait2(g, half, True)
+        wait2(g, half, 1)
         hall_row, half_row, _, n = rows_of(g, half, 0, 2)
 
         def body(i):
@@ -384,48 +416,33 @@
 
         blocks(n, body)
 
-    def compute(g, services):
+    def compute(g, order, segments, bounds, services):
         r0, rows = GROUPS[g]
 
-        def body(i, carry):
+        def product(_, carry):
             deltas_y, deltas_z = carry
-            dy, dz = deltas_y % SIDE, deltas_z % SIDE
-            yt, zt = at(y, dy), at(z, dz)
+            yt, zt = at(y, deltas_y % SIDE), at(z, deltas_z % SIDE)
             column = pl.multiple_of((zt * SIDE + yt) * TILE, TILE)
             acc = jnp.dot(
                 hall[pl.ds(r0, rows), :], virt[:, pl.ds(column, TILE)], preferred_element_type=F32
             )
             part[zt, yt, pl.ds(r0, rows), :] = acc.astype(BF16)
-            for half, d, target, t in ((0, dy, yt, zt), (1, dz, zt, yt)):
-
-                @pl.when(d == 2)
-                def _():
-                    message1(g, half, 0, target, t).start()
-                    message1(g, half, 1, target, t).start()
-
-                @pl.when(d % 2 == 1)
-                def _():
-                    neighbour1(g, half, d // 2, target, t).start()
-
-            @pl.when(i % 2 == 1)
-            def _():
-                services(i)
-
             return deltas_y // SIDE, deltas_z // SIDE
 
-        lax.fori_loop(
-            0,
-            SIDE * SIDE,
-            body,
-            (
-                jnp.int32(sum(d << (2 * i) for i, (d, _) in enumerate(ORDER))),
-                jnp.int32(sum(d << (2 * i) for i, (_, d) in enumerate(ORDER))),
-            ),
-        )
-
-    def both(function, g, *rest):
+        def segment(s, carry):
+            low, high = bounds(s)
+            after = lax.fori_loop(low, high, product, carry)
+            services(s)
+            return after
+
+        packed = [
+            jnp.int32(sum(pair[k] << (2 * i) for i, pair in enumerate(order))) for k in range(2)
+        ]
+        lax.fori_loop(0, segments, segment, tuple(packed))
+
+    def both(function, *rest):
         for half in range(2):
-            function(g, half, *rest)
+            function(*rest[:1], half, *rest[1:])
 
     def loop(n, function):
         lax.fori_loop(0, n, function, 0)
@@ -440,57 +457,113 @@
     def when(condition, name, function):
         pl.when(condition)(scoped(name, function))
 
+    with jax.named_scope("t_near0"):
+        forward_near(0, 0)
     with jax.named_scope("t_part0"):
         all_arrived(0, 0)
     with jax.named_scope("t_virt"):
-        for copy in virt_copies:
-            copy.wait()
-
-    def services0(i):
-        when(i < 8, "t_near", lambda: forward_near(i // 2, 0))
-        when(i == 13, "t_far", lambda: loop(PIECES, forward_far))
+        virt_copy(2).wait()
+
+    def starts(half, *messages):
+        here = ring(half, 0)[0]
+
+        def run():
+            for j in messages:
+                bulk(half, j, at(here, (2, 2, 1, 1, 3, 3)[j])).start()
+
+        return run
+
+    def services0(s):
+        when(
+            s == 0,
+            "t_s0",
+            lambda: (
+                starts(1, 0, 1)(),
+                [virt_copy(delta).wait() for delta in (1, 3, 0)],
+                forward_near(1, 0),
+                forward_near(2, 0),
+            ),
+        )
+        when(s == 1, "t_s1", lambda: (starts(0, 0, 1)(), forward_near(3, 0)))
+        when(s == 2, "t_s2", lambda: (starts(1, 2)(), loop(1, forward_far)))
+        when(s == 3, "t_s3", lambda: (starts(1, 4)(), forward_far(1, 0), forward_far(2, 0)))
+        when(s == 4, "t_s4", starts(0, 2, 4))
 
     with jax.named_scope("t_C0"):
-        compute(0, services0)
+        compute(0, ORDER0, 5, lambda s: (jnp.where(s == 0, 0, 1 + 3 * s), 4 + 3 * s), services0)
+    with jax.named_scope("t_far23"):
+        forward_far(3, 0)
     with jax.named_scope("t_relay0"):
-        for delta in range(SIDE):
-            both(relay1, 0, delta)
+        relay0(0)
+        relay0(1)
     with jax.named_scope("t_part1"):
         all_arrived(3, 2)
         all_arrived(4, 1)
         all_arrived(6, 3)
 
     def middle0():
-        for delta in (2, 1, 3, 0):
-            both(middle, 0, delta)
-
-    def relays():
-        for delta in (1, 3):
-            both(relay1, 1, delta)
-
-    def services1(i):
-        when(i == 5, "t_mid0", middle0)
-        when(i == 9, "t_rel2", lambda: both(relay1, 1, 2))
-        when(i == 11, "t_relay20", lambda: both(relay2, 0))
-        when(i == 13, "t_rel13", relays)
-        when(i == 15, "t_mid2", lambda: both(middle, 1, 2))
+        for half in range(2):
+            wait0(half, 1)
+            for delta in (2, 1, 3, 0):
+                middle(0, half, delta)
+
+    def relays(*deltas):
+        for delta in deltas:
+            for half in range(2):
+                relay1(half, delta)
+
+    def bounds1(s):
+        return jnp.where(s < 2, s, 2 * s - 2), jnp.where(s < 2, s + 1, 2 * s)
+
+    then1 = {
+        3: lambda: relays(2),
+        5: lambda: relays(1, 3),
+        6: lambda: both(middle, 1, 2),
+        8: middle0,
+    }
+
+    def services1(s):
+        def run(k):
+            def go():
+                for i in (k,) if k < 2 else (2 * k - 2, 2 * k - 1):
+                    send_chunk(*ORDER1[i])
+                if k in then1:
+                    with jax.named_scope(f"t_then{k}"):
+                        then1[k]()
+
+            return go
+
+        @pl.when(s < 4)
+        def _():
+            for k in range(4):
+                when(s == k, f"t_s1{k}", run(k))
+
+        @pl.when(s >= 4)
+        def _():
+            for k in range(4, 9):
+                when(s == k, f"t_s1{k}", run(k))
 
     with jax.named_scope("t_C1"):
-        compute(1, services1)
+        compute(1, ORDER1, 9, bounds1, services1)
     with jax.named_scope("t_rel0"):
-        both(relay1, 1, 0)
-    with jax.named_scope("t_mid1"):
+        relays(0)
+    with jax.named_scope("t_mid13"):
         both(middle, 1, 1)
-    with jax.named_scope("t_mid3"):
         both(middle, 1, 3)
     with jax.named_scope("t_relay21"):
         both(relay2, 1)
-    with jax.named_scope("t_fin0"):
-        both(finish, 0)
+    with jax.named_scope("t_relay20"):
+        both(relay2, 0)
     with jax.named_scope("t_midown"):
         both(middle, 1, 0)
     with jax.named_scope("t_fin1"):
         both(finish, 1)
+    with jax.named_scope("t_fin0"):
+        both(finish, 0)
+    with jax.named_scope("t_out"):
+        out_copy = pltpu.make_async_copy(out_ref, out_hbm, isem.at[0])
+        out_copy.start()
+        out_copy.wait()
 
     with jax.named_scope("t_sends"):
         for j, ref in enumerate(
@@ -505,9 +578,10 @@
     rows_first = pl.pallas_call(
         kernel,
         out_shape=jax.ShapeDtypeStruct((512, TILE), BF16),
-        in_specs=[anywhere] * 5,
-        out_specs=pl.BlockSpec(memory_space=pltpu.VMEM),
+        in_specs=[pl.BlockSpec(memory_space=pltpu.HBM)] * 5,
+        out_specs=anywhere,
         scratch_shapes=[
+            pltpu.VMEM((512, TILE), BF16),
             pltpu.SMEM((1, 2, PAIR_CAP), jnp.int32),
             pltpu.SMEM((1, 1), jnp.int32),
             pltpu.VMEM((Q, PAIR_CAP, BB, BB), BF16),
@@ -518,8 +592,9 @@
             pltpu.VMEM((BB, PAIR_CAP * BB), BF16),
             pltpu.VMEM((512, ROWS), BF16),
             pltpu.VMEM((SIDE, SIDE, 512, TILE), BF16),
-            pltpu.VMEM((2, 2, SIDE, 128, TILE), BF16),
-            pltpu.VMEM((2, 2, SIDE, 256, TILE), BF16),
+            pltpu.VMEM((2, 2, SIDE, 32, TILE), BF16),
+            pltpu.VMEM((2, 2, SIDE, 64, TILE), BF16),
+            pltpu.VMEM((2, 2, SIDE, 288, TILE), BF16),
             pltpu.VMEM((2, SIDE, 256, TILE), BF16),
             pltpu.VMEM((2, 256, TILE), F32),
             pltpu.VMEM((2, 2, 128, TILE), BF16),
@@ -531,13 +606,12 @@
             pltpu.SemaphoreType.DMA((2,)),
             pltpu.SemaphoreType.DMA((3, PIECES)),
             pltpu.SemaphoreType.DMA((4,)),
-            pltpu.SemaphoreType.DMA((groups, 2, SIDE)),
-            pltpu.SemaphoreType.DMA((groups, 2, SIDE)),
-            pltpu.SemaphoreType.DMA((groups, 2)),
-            pltpu.SemaphoreType.DMA((groups, 2)),
+            pltpu.SemaphoreType.DMA((2, 2)),
+            pltpu.SemaphoreType.DMA((2, 2, SIDE)),
+            pltpu.SemaphoreType.DMA((2, groups, 2)),
         ],
         compiler_params=pltpu.CompilerParams(
-            collective_id=0, has_side_effects=True, vmem_limit_bytes=60 << 20
+            collective_id=0, has_side_effects=True, vmem_limit_bytes=44 << 20
         ),
         name="occupied_batch",
     )(jnp.swapaxes(pair_map, 1, 2), pair_count, v_blocks, occ_coef, virt_coef)

time: 52 us -> 50.6 us (0.973)
  Pallas kernels: 49.4 us -> 47.2 us
    pallas_call x1, Pallas kernels: 49.4 us -> 47.2 us  [local(): pl.pallas_call(kernel, out_shape=jax.ShapeDtypeStruct((512, TILE), BF16),...]
    unnamed x0 -> x4, local copies, waits for them, and re-layouts: none -> 1.42 us
    transpose x1, local copies, waits for them, and re-layouts: 1.8 us -> 0.84 us  [local(): return rows_first.T]
where the time goes in v3:
time: 50.6 us; the launch traced here: 50.1 us
  Pallas kernels  47.2 us (93%)
  local copies, waits for them, and re-layouts  2.27 us (4%)
  between operations  0.67 us (1%)
    pallas_call x1, Pallas kernels, local(): pl.pallas_call(kernel, out_shape=jax.ShapeDtypeStruct((512, TILE), BF16),...  47.2 us
    unnamed x4, local copies, waits for them, and re-layouts  1.42 us

profile of v3, /device:TPU:0, one launch (start us, length us, event | category | flops | bytes accessed | tf_op | source)
XLA Modules:
  0.0 50.1 jit_solution(8076757812261088870)
XLA Ops:
  0.7 0.0 copy-start
  0.7 0.7 %copy-done = bf16[8,1920]{1,0:T(8,128)(2,1)S(1)} copy-done((bf16[8,1920]{1,0:T(8,128)(2,1)S(1)}, bf16[8,1920]{1,0:T(8,128)(2,1)}, u32[]{:S(2)}) %copy-start) | copy-done | bytes 30744
  1.4 0.0 copy-start.1
  1.4 0.7 %copy-done.1 = s32[1,48,2]{1,2,0:T(2,128)S(1)} copy-done((s32[1,48,2]{1,2,0:T(2,128)S(1)}, s32[1,48,2]{1,2,0:T(2,128)}, u32[]{:S(2)}) %copy-start.1) | copy-done | bytes 408
  2.1 47.2 %occupied_batch.1 = bf16[512,256]{1,0:T(8,128)(2,1)S(1)} custom-call(s32[1,2,48]{2,1,0:T(2,128)S(1)} %bitcast.3, s32[1,1]{1,0:T(1,128)S(6)} %copy.7.pc_hbm, bf16[8,48,128,128]{3,2,1,0:T(8,128)(2,1)} %v_hbm.1, bf16[8,1920]{1,0:T(8,128)(2,1)S(1)} %copy-done, bf16[1920,4096]{1,0:T(8,128)(2,1)} %virt_hbm.1), custom_call_target="tpu_custom_call" | custom-call | tf_op jit(solution)/shard_map/occupied_batch/pallas_call | solution.py:578
  49.3 0.8 %copy.6 = bf16[256,512]{1,0:T(8,128)(2,1)} copy(bf16[256,512]{0,1:T(8,128)(2,1)S(1)} %bitcast.2) | data formatting | bytes 524288 | tf_op jit(solution)/shard_map/transpose | solution.py:618
Async XLA Ops:
  0.7 0.8 %copy-start = (bf16[8,1920]{1,0:T(8,128)(2,1)S(1)}, bf16[8,1920]{1,0:T(8,128)(2,1)}, u32[]{:S(2)}) copy-start(bf16[8,1920]{1,0:T(8,128)(2,1)} %occ_hbm.1) | copy-start | bytes 92164
  1.4 0.7 %copy-start.1 = (s32[1,48,2]{1,2,0:T(2,128)S(1)}, s32[1,48,2]{1,2,0:T(2,128)}, u32[]{:S(2)}) copy-start(s32[1,48,2]{1,2,0:T(2,128)} %param.6) | copy-start | bytes 1156

commit v4 on v3

--- a/solution.py
+++ b/solution.py
@@ -121,8 +121,6 @@
 
     for p in range(PIECES):
         v_copy(p).start()
-    for delta in (2, 1, 3, 0):
-        virt_copy(delta).start()
     with jax.named_scope("t_barrier"):
         pl.semaphore_wait(barrier, len(peers))
 
@@ -141,6 +139,8 @@
     with jax.named_scope("t_small"):
         small[1].wait()
         small[2].wait()
+    for delta in (2, 1, 3, 0):
+        virt_copy(delta).start()
     for j in range(NEAR):
         tab[j] = halo[0, :, j * BB : (j + 1) * BB].astype(F32)
         tab[NEAR + HERE + j] = halo[1, :, j * BB : (j + 1) * BB].astype(F32)
@@ -545,11 +545,11 @@
 
     with jax.named_scope("t_C1"):
         compute(1, ORDER1, 9, bounds1, services1)
-    with jax.named_scope("t_rel0"):
-        relays(0)
     with jax.named_scope("t_mid13"):
         both(middle, 1, 1)
         both(middle, 1, 3)
+    with jax.named_scope("t_rel0"):
+        relays(0)
     with jax.named_scope("t_relay21"):
         both(relay2, 1)
     with jax.named_scope("t_relay20"):

time: 50.6 us -> 50.4 us (level)
  no operation moved by 1% of the time
where the time goes in v4:
time: 50.4 us; the launch traced here: 50.1 us
  Pallas kernels  47.2 us (94%)
  local copies, waits for them, and re-layouts  2.27 us (5%)
  between operations  0.67 us (1%)
    pallas_call x1, Pallas kernels, local(): pl.pallas_call(kernel, out_shape=jax.ShapeDtypeStruct((512, TILE), BF16),...  47.2 us
    unnamed x4, local copies, waits for them, and re-layouts  1.42 us

profile of v4, /device:TPU:0, one launch (start us, length us, event | category | flops | bytes accessed | tf_op | source)
XLA Modules:
  0.0 50.1 jit_solution(1766346627669528188)
XLA Ops:
  0.7 0.0 copy-start
  0.7 0.7 %copy-done = bf16[8,1920]{1,0:T(8,128)(2,1)S(1)} copy-done((bf16[8,1920]{1,0:T(8,128)(2,1)S(1)}, bf16[8,1920]{1,0:T(8,128)(2,1)}, u32[]{:S(2)}) %copy-start) | copy-done | bytes 30744
  1.4 0.0 copy-start.1
  1.4 0.7 %copy-done.1 = s32[1,48,2]{1,2,0:T(2,128)S(1)} copy-done((s32[1,48,2]{1,2,0:T(2,128)S(1)}, s32[1,48,2]{1,2,0:T(2,128)}, u32[]{:S(2)}) %copy-start.1) | copy-done | bytes 408
  2.1 47.2 %occupied_batch.1 = bf16[512,256]{1,0:T(8,128)(2,1)S(1)} custom-call(s32[1,2,48]{2,1,0:T(2,128)S(1)} %bitcast.3, s32[1,1]{1,0:T(1,128)S(6)} %copy.7.pc_hbm, bf16[8,48,128,128]{3,2,1,0:T(8,128)(2,1)} %v_hbm.1, bf16[8,1920]{1,0:T(8,128)(2,1)S(1)} %copy-done, bf16[1920,4096]{1,0:T(8,128)(2,1)} %virt_hbm.1), custom_call_target="tpu_custom_call" | custom-call | tf_op jit(solution)/shard_map/occupied_batch/pallas_call | solution.py:578
  49.3 0.8 %copy.6 = bf16[256,512]{1,0:T(8,128)(2,1)} copy(bf16[256,512]{0,1:T(8,128)(2,1)S(1)} %bitcast.2) | data formatting | bytes 524288 | tf_op jit(solution)/shard_map/transpose | solution.py:618
Async XLA Ops:
  0.7 0.8 %copy-start = (bf16[8,1920]{1,0:T(8,128)(2,1)S(1)}, bf16[8,1920]{1,0:T(8,128)(2,1)}, u32[]{:S(2)}) copy-start(bf16[8,1920]{1,0:T(8,128)(2,1)} %occ_hbm.1) | copy-start | bytes 92164
  1.4 0.7 %copy-start.1 = (s32[1,48,2]{1,2,0:T(2,128)S(1)}, s32[1,48,2]{1,2,0:T(2,128)}, u32[]{:S(2)}) copy-start(s32[1,48,2]{1,2,0:T(2,128)} %param.6) | copy-start | bytes 1156

commit v5 on v4

--- a/solution.py
+++ b/solution.py
@@ -315,12 +315,15 @@
             ref = rel2.at[half, :, pl.ds(quarter_row, n)]
         remote(ref, ref, sends.at[3], m2.at[landing, g, half], ring(half, 1)[1]).wait_recv()
 
-    def blocks(n, body):
+    def rows_by(size, start, i):
+        return pl.ds(pl.multiple_of(start + i, 32), size)
+
+    def blocks(n, body, size=32):
         def step(i, _):
-            body(i * 32)
+            body(i * size)
             return 0
 
-        lax.fori_loop(0, n // 32, step, 0)
+        lax.fori_loop(0, n // size, step, 0)
 
     def rows32(start, i):
         return pl.ds(pl.multiple_of(start + i, 32), 32)
@@ -335,12 +338,12 @@
             row = R0 + (2 * half + way) * QUARTER
 
             def body(i):
-                total = part[zt, yt, rows32(row, i), :].astype(F32) + in1[
-                    half, way, t, rows32(2 * QUARTER, i), :
+                total = part[zt, yt, rows_by(QUARTER, row, i), :].astype(F32) + in1[
+                    half, way, t, rows_by(QUARTER, 2 * QUARTER, i), :
                 ].astype(F32)
-                part[zt, yt, rows32(row, i), :] = total.astype(BF16)
-
-            blocks(QUARTER, body)
+                part[zt, yt, rows_by(QUARTER, row, i), :] = total.astype(BF16)
+
+            blocks(QUARTER, body, QUARTER)
             single(half, way, way, 1, target, t).start()
 
     def relay0(half):
@@ -369,16 +372,16 @@
 
         def body(i):
             total = (
-                part[zt, yt, rows32(hall_row, i), :].astype(F32)
-                + landed[half, 0, t, rows32(0, i), :].astype(F32)
-                + landed[half, 1, t, rows32(0, i), :].astype(F32)
+                part[zt, yt, rows_by(GROUPS[g][1] // 4, hall_row, i), :].astype(F32)
+                + landed[half, 0, t, rows_by(GROUPS[g][1] // 4, 0, i), :].astype(F32)
+                + landed[half, 1, t, rows_by(GROUPS[g][1] // 4, 0, i), :].astype(F32)
             )
             if delta:
-                tsum[half, t, rows32(half_row, i), :] = total.astype(BF16)
+                tsum[half, t, rows_by(GROUPS[g][1] // 4, half_row, i), :] = total.astype(BF16)
             else:
-                own[half, rows32(half_row, i), :] = total
-
-        blocks(n, body)
+                own[half, rows_by(GROUPS[g][1] // 4, half_row, i), :] = total
+
+        blocks(n, body, GROUPS[g][1] // 4)
         for j in {0: (), 1: (2,), 2: (0, 1), 3: (4,)}[delta]:
             message2(g, half, j, t).start()
 
@@ -390,12 +393,12 @@
             _, half_row, quarter_row, n = rows_of(g, half, way)
 
             def body(i):
-                total = tsum[half, target, rows32(half_row, i), :].astype(F32) + rel2[
-                    half, way, rows32(quarter_row, i), :
+                total = tsum[half, target, rows_by(GROUPS[g][1] // 4, half_row, i), :].astype(F32) + rel2[
+                    half, way, rows_by(GROUPS[g][1] // 4, quarter_row, i), :
                 ].astype(F32)
-                tsum[half, target, rows32(half_row, i), :] = total.astype(BF16)
-
-            blocks(n, body)
+                tsum[half, target, rows_by(GROUPS[g][1] // 4, half_row, i), :] = total.astype(BF16)
+
+            blocks(n, body, GROUPS[g][1] // 4)
             message2(g, half, onward, target).start()
 
     def finish(g, half):

time: 50.4 us -> 50.3 us (level)
  no operation moved by 1% of the time
where the time goes in v5:
time: 50.3 us; the launch traced here: 50.1 us
  Pallas kernels  47.1 us (94%)
  local copies, waits for them, and re-layouts  2.27 us (5%)
  between operations  0.67 us (1%)
    pallas_call x1, Pallas kernels, local(): pl.pallas_call(kernel, out_shape=jax.ShapeDtypeStruct((512, TILE), BF16),...  47.1 us
    unnamed x4, local copies, waits for them, and re-layouts  1.42 us

profile of v5, /device:TPU:0, one launch (start us, length us, event | category | flops | bytes accessed | tf_op | source)
XLA Modules:
  0.0 50.1 jit_solution(13902984896690251065)
XLA Ops:
  0.7 0.0 copy-start
  0.7 0.7 %copy-done = bf16[8,1920]{1,0:T(8,128)(2,1)S(1)} copy-done((bf16[8,1920]{1,0:T(8,128)(2,1)S(1)}, bf16[8,1920]{1,0:T(8,128)(2,1)}, u32[]{:S(2)}) %copy-start) | copy-done | bytes 30744
  1.4 0.0 copy-start.1
  1.4 0.7 %copy-done.1 = s32[1,48,2]{1,2,0:T(2,128)S(1)} copy-done((s32[1,48,2]{1,2,0:T(2,128)S(1)}, s32[1,48,2]{1,2,0:T(2,128)}, u32[]{:S(2)}) %copy-start.1) | copy-done | bytes 408
  2.1 47.1 %occupied_batch.1 = bf16[512,256]{1,0:T(8,128)(2,1)S(1)} custom-call(s32[1,2,48]{2,1,0:T(2,128)S(1)} %bitcast.3, s32[1,1]{1,0:T(1,128)S(6)} %copy.7.pc_hbm, bf16[8,48,128,128]{3,2,1,0:T(8,128)(2,1)} %v_hbm.1, bf16[8,1920]{1,0:T(8,128)(2,1)S(1)} %copy-done, bf16[1920,4096]{1,0:T(8,128)(2,1)} %virt_hbm.1), custom_call_target="tpu_custom_call" | custom-call | tf_op jit(solution)/shard_map/occupied_batch/pallas_call | solution.py:581
  49.2 0.8 %copy.6 = bf16[256,512]{1,0:T(8,128)(2,1)} copy(bf16[256,512]{0,1:T(8,128)(2,1)S(1)} %bitcast.2) | data formatting | bytes 524288 | tf_op jit(solution)/shard_map/transpose | solution.py:621
Async XLA Ops:
  0.7 0.8 %copy-start = (bf16[8,1920]{1,0:T(8,128)(2,1)S(1)}, bf16[8,1920]{1,0:T(8,128)(2,1)}, u32[]{:S(2)}) copy-start(bf16[8,1920]{1,0:T(8,128)(2,1)} %occ_hbm.1) | copy-start | bytes 92164
  1.4 0.7 %copy-start.1 = (s32[1,48,2]{1,2,0:T(2,128)S(1)}, s32[1,48,2]{1,2,0:T(2,128)}, u32[]{:S(2)}) copy-start(s32[1,48,2]{1,2,0:T(2,128)} %param.6) | copy-start | bytes 1156
